TPU v7x, 32 devices: a whole 2x2x4 slice. The times are simulated.
32 devices in a mesh: pipe: 2 (over x), expert: 16 (over z, y, core).
Axes of the slice: x: 2, y: 2, z: 4, core: 2. Of those that a mesh axis runs over, the one named last changes fastest.
Arguments:
- tokens: bfloat16 [2048, 1024], P('expert'), may hold values from -6 to 6
- out_grad: bfloat16 [2048, 1024], P('expert'), may hold values from -6 to 6
- routes: int32 [2048, 6], P('expert'), may hold values from 0 to 15, as said below
- slots: int32 [2048, 6], P('expert'), may hold values from 0 to 63, as said below
- gates: bfloat16 [2048, 6], P('expert'), may hold values from 0.099609375 to 1
- w_gate: bfloat16 [16, 1408, 1024], P('expert', 'pipe'), may hold values from -0.1875 to 0.1875
- w_up: bfloat16 [16, 1408, 1024], P('expert', 'pipe'), may hold values from -0.1875 to 0.1875
- w_down: bfloat16 [16, 1408, 1024], P('expert', 'pipe'), may hold values from -0.15625 to 0.15625
Outputs:
- mixed: bfloat16 [2048, 1024], P('expert', 'pipe')
- grad_tokens: bfloat16 [2048, 1024], P('expert', 'pipe')
- grad_gates: float32 [2048, 6], P('expert')
- grad_w_gate: bfloat16 [16, 1408, 1024], P('expert', 'pipe')
- grad_w_up: bfloat16 [16, 1408, 1024], P('expert', 'pipe')
- grad_w_down: bfloat16 [16, 1408, 1024], P('expert', 'pipe')
Inputs may be any that keep to these rules, and one draw needn't show every extreme that they name: `routes`: each token names 6 different experts. Within one device's block of 128 tokens no expert is named more than 64 times, and some expert is named exactly 64 times by every block. Within one block of 128 tokens the pairs (routes, slots) are all different.
All inputs are finite; a program needn't handle non-finite values.
Results may differ from a plain program's by a relative error of at most 0.015.
Values may be sent and summed in bfloat16 or wider, within the bound.
A program may use at most 64 MiB of HBM per device.

v0:
```python
import jax
import jax.numpy as jnp
from jax import lax
from jax.sharding import PartitionSpec as P


def expert_forward(arrived_x, gate_w, up_w, down_w):
    contract = (((1,), (1,)), ((), ()))
    gate_pre = lax.dot_general(arrived_x, gate_w, contract, preferred_element_type=jnp.float32)
    up_pre = lax.dot_general(arrived_x, up_w, contract, preferred_element_type=jnp.float32)
    sigma = jax.nn.sigmoid(gate_pre)
    silu_val = gate_pre * sigma
    act = (silu_val * up_pre).astype(jnp.bfloat16)
    partial_out = jnp.dot(act, down_w, preferred_element_type=jnp.float32).astype(jnp.bfloat16)
    return (partial_out, (gate_pre, up_pre, sigma, silu_val, act))


def expert_backward(arrived_x, arrived_dy, arrived_g, saved, gate_w, up_w, down_w):
    gate_pre, up_pre, sigma, silu_val, act = saved
    contract = (((1,), (1,)), ((), ()))
    over_rows = (((0,), (0,)), ((), ()))
    d_out = (arrived_g.astype(jnp.float32)[:, None] * arrived_dy.astype(jnp.float32)).astype(
        jnp.bfloat16
    )
    d_act = lax.dot_general(d_out, down_w, contract, preferred_element_type=jnp.float32)
    d_gate = (d_act * up_pre * sigma * (1.0 + gate_pre * (1.0 - sigma))).astype(jnp.bfloat16)
    d_up = (d_act * silu_val).astype(jnp.bfloat16)
    partial_back = (
        jnp.dot(d_gate, gate_w, preferred_element_type=jnp.float32)
        + jnp.dot(d_up, up_w, preferred_element_type=jnp.float32)
    ).astype(jnp.bfloat16)
    grad_gate_w = lax.dot_general(
        d_gate, arrived_x, over_rows, preferred_element_type=jnp.float32
    ).astype(jnp.bfloat16)
    grad_up_w = lax.dot_general(
        d_up, arrived_x, over_rows, preferred_element_type=jnp.float32
    ).astype(jnp.bfloat16)
    grad_down_w = lax.dot_general(act, d_out, over_rows, preferred_element_type=jnp.float32).astype(
        jnp.bfloat16
    )
    return (partial_back, (grad_gate_w[None], grad_up_w[None], grad_down_w[None]))


def pick_rows(returned, flat_slot, local_tokens, topk):
    slot_total = returned.shape[0] * returned.shape[1]
    flat_back = returned.reshape(slot_total, returned.shape[2])
    return jnp.take(flat_back, flat_slot, axis=0).reshape(local_tokens, topk, returned.shape[2])


def body(tokens, out_grad, routes, slots, gates, w_gate, w_up, w_down):
    local_tokens = tokens.shape[0]
    topk = routes.shape[1]
    sources = lax.axis_size("expert")
    experts = sources * w_gate.shape[0]
    capacity = 4 * local_tokens * topk // (3 * experts)
    slot_total = experts * capacity
    flat_slot = (routes * capacity + slots).reshape(-1)
    owner_token = jnp.arange(local_tokens * topk, dtype=jnp.int32) // topk
    owner = jnp.full((slot_total,), local_tokens, jnp.int32).at[flat_slot].set(owner_token)
    gate_slot = (
        jnp.zeros((slot_total,), jnp.bfloat16)
        .at[flat_slot]
        .set(gates.reshape(-1))
        .reshape(experts, capacity)
    )
    share = tokens.shape[1] // lax.axis_size("pipe")
    begin = lax.axis_index("pipe") * share

    def fill_rows(matrix):
        taken = jnp.take(matrix, owner, axis=0, mode="fill", fill_value=0)
        return taken.reshape(experts, capacity, matrix.shape[1])

    x_share = lax.dynamic_slice_in_dim(tokens, begin, share, 1)
    dy_share = lax.dynamic_slice_in_dim(out_grad, begin, share, 1)
    part_x, part_dy, arrived_g = (
        lax.all_to_all(fill_rows(x_share), "expert", split_axis=0, concat_axis=0, tiled=True),
        lax.all_to_all(fill_rows(dy_share), "expert", split_axis=0, concat_axis=0, tiled=True),
        lax.all_to_all(gate_slot, "expert", split_axis=0, concat_axis=0, tiled=True),
    )
    arrived_x, arrived_dy = (
        lax.all_gather(part_x, "pipe", axis=2, tiled=True),
        lax.all_gather(part_dy, "pipe", axis=2, tiled=True),
    )
    row_count = sources * capacity
    width = arrived_x.shape[2]
    arrived_x = arrived_x.reshape(row_count, width)
    arrived_dy = arrived_dy.reshape(row_count, width)
    arrived_g = arrived_g.reshape(row_count)
    gate_w = w_gate[0]
    up_w = w_up[0]
    down_w = w_down[0]
    ones_weight = jnp.ones((local_tokens, topk), jnp.bfloat16)
    batch_k = (((1,), (1,)), ((0,), (0,)))
    batch_d = (((2,), (1,)), ((0,), (0,)))
    partial_out, saved = expert_forward(arrived_x, gate_w, up_w, down_w)
    out_back = lax.all_to_all(
        partial_out.reshape(sources, capacity, width),
        "expert",
        split_axis=0,
        concat_axis=0,
        tiled=True,
    )
    picked = pick_rows(out_back, flat_slot, local_tokens, topk)
    mixed_part = lax.dot_general(gates, picked, batch_k, preferred_element_type=jnp.float32)
    gate_part = lax.dot_general(picked, out_grad, batch_d, preferred_element_type=jnp.float32)
    mixed_sum = lax.psum_scatter(
        mixed_part.astype(jnp.bfloat16), "pipe", scatter_dimension=1, tiled=True
    )
    partial_back, weight_grads = expert_backward(
        arrived_x, arrived_dy, arrived_g, saved, gate_w, up_w, down_w
    )
    grad_back = lax.all_to_all(
        partial_back.reshape(sources, capacity, width),
        "expert",
        split_axis=0,
        concat_axis=0,
        tiled=True,
    )
    picked_grad = pick_rows(grad_back, flat_slot, local_tokens, topk)
    grad_part = lax.dot_general(
        ones_weight, picked_grad, batch_k, preferred_element_type=jnp.float32
    )
    grad_total = lax.psum_scatter(
        grad_part.astype(jnp.bfloat16), "pipe", scatter_dimension=1, tiled=True
    )
    grad_gates = lax.psum(gate_part, "pipe")
    return (mixed_sum, grad_total, grad_gates, weight_grads[0], weight_grads[1], weight_grads[2])


def solution(mesh):
    return jax.shard_map(
        body,
        mesh=mesh,
        in_specs=(
            P("expert", None),
            P("expert", None),
            P("expert", None),
            P("expert", None),
            P("expert", None),
            P("expert", "pipe", None),
            P("expert", "pipe", None),
            P("expert", "pipe", None),
        ),
        out_specs=(
            P("expert", "pipe"),
            P("expert", "pipe"),
            P("expert", None),
            P("expert", "pipe", None),
            P("expert", "pipe", None),
            P("expert", "pipe", None),
        ),
        check_vma=False,
    )
```

profile of v0, /device:TPU:0, one launch (start us, length us, event | category | flops | bytes accessed | tf_op | source)
XLA Modules:
  0.0 287.2 jit_solution(10772181095873960082)
XLA Ops:
  7.2 0.8 multiply_add_fusion
  8.2 0.1 reshape.110
  8.3 3.4 %scatter_custom_fusion = s32[1024]{0:T(1024)S(1)} fusion(s32[768]{0:T(1024)S(1)} %fusion.23, s32[768]{0:T(1024)S(1)} %add_select_fusion, s32[]{:T(128)} %constant.34.clone.1), kind=kCustom, calls=%fused_computation.58 | custom fusion | bytes 4100 | tf_op jit(solution)/shard_map/scatter | solution.py:59
  11.8 1.0 constant_dynamic-slice_fusion
  12.8 4.0 %gather_fusion.2 = bf16[1024,512]{1,0:T(8,128)(2,1)S(1)} fusion(bf16[128,512]{1,0:T(8,128)(2,1)S(1)} %get-tuple-element.15, s32[1024]{0:T(1024)S(1)} %fusion.22), kind=kCustom, calls=%fused_computation.2.clone | custom fusion | bytes 2101248 | tf_op jit(solution)/shard_map/jit(_take)/gather | solution.py:70
  16.7 5.1 %gather_fusion = bf16[1024,512]{1,0:T(8,128)(2,1)} fusion(bf16[128,512]{1,0:T(8,128)(2,1)S(1)} %get-tuple-element.16, s32[1024]{0:T(1024)S(1)} %fusion.22), kind=kCustom, calls=%fused_computation.clone | custom fusion | bytes 2101248 | tf_op jit(solution)/shard_map/jit(_take)/gather | solution.py:70
  21.8 2.4 broadcast_select_fusion.2
  24.2 32.1 %all_to_all.30 = bf16[16,64,512]{2,1,0:T(8,128)(2,1)} all-to-all(bf16[16,64,512]{2,1,0:T(8,128)(2,1)S(1)} %bitcast.65), channel_id=1, replica_groups=mesh['pipe'=2,'expert'=16] {'expert'}, dimensions={0} | all-to-all | bytes 2097152 | tf_op jit(solution)/shard_map/all_to_all | solution.py:76
  56.4 29.6 %all_to_all.31 = bf16[16,64,512]{2,1,0:T(8,128)(2,1)} all-to-all(bf16[16,64,512]{2,1,0:T(8,128)(2,1)S(1)} %bitcast.64), channel_id=1, replica_groups=mesh['pipe'=2,'expert'=16] {'expert'}, dimensions={0} | all-to-all | bytes 2097152 | tf_op jit(solution)/shard_map/all_to_all | solution.py:77
  86.2 0.2 reshape.169
  86.4 8.6 %scatter_custom_fusion.1 = bf16[1024]{0:T(1024)(128)(2,1)S(1)} fusion(s32[768]{0:T(1024)S(1)} %fusion.23, bf16[768]{0:T(1024)(128)(2,1)S(1)} %reshape.169, bf16[]{:T(256)} %constant.22.clone.1), kind=kCustom, calls=%fused_computation.60 | custom fusion | bytes 2050 | tf_op jit(solution)/shard_map/scatter | solution.py:63
  95.1 11.2 %all_to_all.32 = bf16[16,1,64]{2,1,0:T(2,128)(2,1)S(1)} all-to-all(bf16[16,1,64]{2,1,0:T(2,128)(2,1)S(1)} %all_to_all.24), channel_id=1, replica_groups=mesh['pipe'=2,'expert'=16] {'expert'}, dimensions={0} | all-to-all | bytes 4096 | tf_op jit(solution)/shard_map/all_to_all | solution.py:78
  106.4 5.4 %fusion.9 = f32[1024,704]{0,1:T(8,128)} fusion(bf16[1024,1024]{1,0:T(8,128)(2,1)} %bitcast.75, bf16[1,704,1024]{2,1,0:T(8,128)(2,1)} %param.18), kind=kOutput, calls=%fused_computation.28 | convolution fusion | flops 1476395008 | bytes 6422528 | tf_op jit(solution)/shard_map/dot_general | solution.py:10
  111.8 3.3 %fusion.13 = f32[1024,704]{0,1:T(8,128)} fusion(bf16[1024,1024]{1,0:T(8,128)(2,1)S(1)} %bitcast.77, bf16[1,704,1024]{2,1,0:T(8,128)(2,1)S(1)} %copy-done.9), kind=kOutput, calls=%fused_computation.32 | convolution fusion | flops 1476395008 | bytes 6422528 | tf_op jit(solution)/shard_map/dot_general | solution.py:9
  115.1 9.6 %all-gather.5.cloned.1.call-done = bf16[16,64,1024]{2,1,0:T(8,128)(2,1)} async-done(((bf16[16,64,512]{2,1,0:T(8,128)(2,1)}), bf16[16,64,1024]{2,1,0:T(8,128)(2,1)}) %all-gather.5.cloned.1.call-update) | async-done | bytes 2097168 | tf_op jit(solution)/shard_map/all_gather | solution.py:82
  124.7 2.1 multiply_convert_fusion
  126.8 0.3 copy-done.11
  127.1 5.4 %multiply_convert_fusion.1 = (bf16[1024,704]{0,1:T(8,128)(2,1)}, bf16[1024,704]{0,1:T(8,128)(2,1)}, bf16[1024,704]{0,1:T(8,128)(2,1)S(1)}) fusion(f32[1024,704]{0,1:T(8,128)} %fusion.13, f32[1024,704]{0,1:T(8,128)S(1)} %copy-done.11, bf16[1024,1024]{1,0:T(8,128)(2,1)S(1)} %bitcast.68, bf16[1,704,1024]{2,1,0:T(8,128)(2,1)S(1)} %copy-done), kind=kOutput, calls=%fused_computation.10 | convolution fusion | flops 1487208448 | bytes 13631488 | tf_op jit(solution)/shard_map/dot_general | solution.py:25
  132.6 3.2 %convolution_convert_fusion = bf16[1024,1024]{1,0:T(8,128)(2,1)} fusion(bf16[1024,704]{0,1:T(8,128)(2,1)S(1)} %get-tuple-element.10, bf16[1,704,1024]{2,1,0:T(8,128)(2,1)S(1)} %copy-done), kind=kOutput, calls=%fused_computation.15 | convolution fusion | flops 1477443584 | bytes 4980736 | tf_op jit(solution)/shard_map/dot_general | solution.py:14
  135.7 5.6 %all-to-all-start.1 = ((bf16[16,64,1024]{2,1,0:T(8,128)(2,1)}), bf16[16,64,1024]{2,1,0:T(8,128)(2,1)S(1)}, u32[]{:S(2)}, u32[]{:S(2)}) async-start(bf16[16,64,1024]{2,1,0:T(8,128)(2,1)} %bitcast.67), calls=%async_computation.1 | async-start | bytes 4194304 | tf_op jit(solution)/shard_map/all_to_all | solution.py:96
  141.4 3.8 %fusion.11 = f32[1024,1024]{1,0:T(8,128)S(1)} fusion(bf16[1024,704]{0,1:T(8,128)(2,1)} %get-tuple-element.9, bf16[1,704,1024]{2,1,0:T(8,128)(2,1)} %param.17), kind=kOutput, calls=%fused_computation.30 | convolution fusion | flops 1476395008 | bytes 7077888 | tf_op jit(solution)/shard_map/dot_general | solution.py:29
  145.2 3.3 %add_convert_fusion = bf16[1024,1024]{1,0:T(8,128)(2,1)} fusion(f32[1024,1024]{1,0:T(8,128)S(1)} %fusion.11, bf16[1024,704]{0,1:T(8,128)(2,1)S(1)} %copy-done.13, bf16[1,704,1024]{2,1,0:T(8,128)(2,1)S(1)} %copy-done.10), kind=kOutput, calls=%fused_computation.8 | convolution fusion | flops 1478492160 | bytes 9175040 | tf_op jit(solution)/shard_map/dot_general | solution.py:30
  148.5 33.8 %all-to-all-done.1 = bf16[16,64,1024]{2,1,0:T(8,128)(2,1)S(1)} async-done(((bf16[16,64,1024]{2,1,0:T(8,128)(2,1)}), bf16[16,64,1024]{2,1,0:T(8,128)(2,1)S(1)}, u32[]{:S(2)}, u32[]{:S(2)}) %all-to-all-start.1) | async-done | bytes 2097184 | tf_op jit(solution)/shard_map/all_to_all | solution.py:96
  182.3 11.3 %all-to-all-start.4 = ((bf16[16,64,1024]{2,1,0:T(8,128)(2,1)}), bf16[16,64,1024]{2,1,0:T(8,128)(2,1)}, u32[]{:S(2)}, u32[]{:S(2)}) async-start(bf16[16,64,1024]{2,1,0:T(8,128)(2,1)} %bitcast.66), calls=%async_computation.5 | async-start | bytes 4194304 | tf_op jit(solution)/shard_map/all_to_all | solution.py:112
  193.6 0.3 reduce-scatter.5.cloned.1.call-start
  193.9 1.0 reshape.115
  194.9 0.8 copy.24
  195.6 0.6 compare_and_fusion
  196.2 0.6 convert_reduce_fusion
  196.8 0.8 reshape.123
  197.6 4.9 %fusion.3 = bf16[1,704,1024]{2,1,0:T(8,128)(2,1)} fusion(bf16[1024,704]{0,1:T(8,128)(2,1)} %get-tuple-element.8, bf16[1024,1024]{1,0:T(8,128)(2,1)} %bitcast.76), kind=kOutput, calls=%fused_computation.22 | convolution fusion | flops 1477115904 | bytes 4980736 | tf_op jit(solution)/shard_map/dot_general | solution.py:35
  202.5 2.8 fusion.2
  205.3 3.6 %gather_fusion.1 = bf16[768,1024]{1,0:T(8,128)(2,1)} fusion(bf16[1024,1024]{1,0:T(8,128)(2,1)S(1)} %bitcast.63, s32[1024]{0:T(1024)S(1)} %pad_clamp_fusion), kind=kCustom, calls=%fused_computation.1.clone | custom fusion | bytes 3148800 | tf_op jit(solution)/shard_map/jit(_take)/gather | solution.py:47
  208.9 25.7 %all-to-all-done.4 = bf16[16,64,1024]{2,1,0:T(8,128)(2,1)} async-done(((bf16[16,64,1024]{2,1,0:T(8,128)(2,1)}), bf16[16,64,1024]{2,1,0:T(8,128)(2,1)}, u32[]{:S(2)}, u32[]{:S(2)}) %all-to-all-start.4) | async-done | bytes 2097184 | tf_op jit(solution)/shard_map/all_to_all | solution.py:112
  234.7 6.6 %gather_fusion.3 = bf16[768,1024]{1,0:T(8,128)(2,1)} fusion(bf16[1024,1024]{1,0:T(8,128)(2,1)} %bitcast.13, s32[1024]{0:T(1024)S(1)} %pad_clamp_fusion), kind=kCustom, calls=%fused_computation.3.clone | custom fusion | bytes 3148800 | tf_op jit(solution)/shard_map/jit(_take)/gather | solution.py:47
  241.2 3.5 %broadcast_select_fusion = (bf16[768,1024]{1,0:T(8,128)(2,1)}, bf16[768,1024]{1,0:T(8,128)(2,1)}) fusion(bf16[768,1024]{1,0:T(8,128)(2,1)} %gather_fusion.3, pred[768]{0:T(1024)(128)(4,1)S(1)} %copy-done.6, bf16[768,1024]{1,0:T(8,128)(2,1)S(1)} %copy-done.1), kind=kLoop, calls=%fused_computation.19 | loop fusion | flops 1572864 | bytes 6292224 | tf_op jit(solution)/shard_map/jit(_take)/select_n | solution.py:47
  244.7 2.5 reshape.121
  247.2 0.7 fusion.17
  247.9 0.8 copy.34
  248.8 3.3 %fusion = bf16[1024,1024]{1,0:T(8,128)(2,1)} fusion(f32[1024]{0:T(1024)S(1)} %reshape.123, bf16[16,64,1024]{2,1,0:T(8,128)(2,1)} %all-gather.5.cloned.1.call-done), kind=kLoop, calls=%fused_computation.7 | loop fusion | flops 3145728 | bytes 4198400 | tf_op jit(solution)/shard_map/convert_element_type | solution.py:22
  252.1 2.5 reshape.116
  254.6 1.5 fusion.29
  256.1 0.8 copy.35
  257.0 4.8 %fusion.4 = bf16[1,704,1024]{2,1,0:T(8,128)(2,1)} fusion(bf16[1024,704]{0,1:T(8,128)(2,1)} %copy-done.14, bf16[1024,1024]{1,0:T(8,128)(2,1)} %fusion), kind=kOutput, calls=%fused_computation.23 | convolution fusion | flops 1477115904 | bytes 4980736 | tf_op jit(solution)/shard_map/dot_general | solution.py:38
  261.8 2.1 fusion.15
  263.8 0.9 copy.29
  264.7 5.5 %psum.7 = f32[128,6]{0,1:T(8,128)} all-reduce(f32[128,6]{0,1:T(8,128)S(1)} %bitcast.73), channel_id=1, replica_groups=mesh['pipe'=2,'expert'=16] {'pipe'}, use_global_device_ids=true, to_apply=%region_4.7 | all-reduce | flops 768 | bytes 6144 | tf_op jit(solution)/shard_map/psum | solution.py:126
  270.3 10.4 %reduce-scatter.3.cloned.1.call-done = bf16[128,512]{1,0:T(8,128)(2,1)} async-done(((bf16[128,1024]{1,0:T(8,128)(2,1)}), bf16[128,512]{1,0:T(8,128)(2,1)}) %reduce-scatter.3.cloned.1.call-update) | async-done | bytes 131088 | tf_op jit(solution)/shard_map/reduce_scatter | solution.py:106
  (48 shorter events, 0.7 us)
Async XLA Ops:
  7.2 119.7 %copy-start = (bf16[1,704,1024]{2,1,0:T(8,128)(2,1)S(1)}, bf16[1,704,1024]{2,1,0:T(8,128)(2,1)}, u32[]{:S(2)}) copy-start(bf16[1,704,1024]{2,1,0:T(8,128)(2,1)} %param.19) | copy-start | bytes 4325380
  7.2 99.2 %all-gather.3.cloned.1.call-start = ((), (), s32[]{:S(2)}) async-start(), calls=%async_computation.7 | async-start | bytes 3145728 | tf_op jit(solution)/shard_map/all_gather | solution.py:81
  8.2 3.6 %copy-start.3 = (s32[128,6]{1,0:T(8,128)}, s32[128,6]{1,0:T(8,128)S(1)}, u32[]{:S(2)}) copy-start(s32[128,6]{1,0:T(8,128)S(1)} %copy.20) | copy-start | bytes 9220
  24.2 32.2 %copy-start.2 = (bf16[1024,512]{1,0:T(8,128)(2,1)S(1)}, bf16[1024,512]{1,0:T(8,128)(2,1)}, u32[]{:S(2)}) copy-start(bf16[1024,512]{1,0:T(8,128)(2,1)} %get-tuple-element.13) | copy-start | bytes 3145732
  56.4 29.7 %copy-start.5 = (bf16[128,6]{0,1:T(8,128)(2,1)S(1)}, bf16[128,6]{0,1:T(8,128)(2,1)}, u32[]{:S(2)}) copy-start(bf16[128,6]{0,1:T(8,128)(2,1)} %param.16) | copy-start | bytes 4612
  56.4 68.3 %all-gather.5.cloned.1.call-start = ((), (), s32[]{:S(2)}) async-start(), calls=%async_computation.9 | async-start | bytes 3145728 | tf_op jit(solution)/shard_map/all_gather | solution.py:82
  106.4 5.5 %copy-start.7 = (bf16[16,64,1024]{2,1,0:T(8,128)(2,1)S(1)}, bf16[16,64,1024]{2,1,0:T(8,128)(2,1)}, u32[]{:S(2)}) copy-start(bf16[16,64,1024]{2,1,0:T(8,128)(2,1)} %all-gather.3.cloned.1.call-done) | copy-start | bytes 6291460
  106.4 5.5 %copy-start.9 = (bf16[1,704,1024]{2,1,0:T(8,128)(2,1)S(1)}, bf16[1,704,1024]{2,1,0:T(8,128)(2,1)}, u32[]{:S(2)}) copy-start(bf16[1,704,1024]{2,1,0:T(8,128)(2,1)} %param.17) | copy-start | bytes 4325380
  124.7 2.4 copy-start.11
  132.6 3.2 %copy-start.14 = (bf16[1024,704]{0,1:T(8,128)(2,1)}, bf16[1024,704]{0,1:T(8,128)(2,1)S(1)}, u32[]{:S(2)}) copy-start(bf16[1024,704]{0,1:T(8,128)(2,1)S(1)} %get-tuple-element.10) | copy-start | bytes 4325380
  135.7 46.6 %all-to-all-start.1 = ((bf16[16,64,1024]{2,1,0:T(8,128)(2,1)}), bf16[16,64,1024]{2,1,0:T(8,128)(2,1)S(1)}, u32[]{:S(2)}, u32[]{:S(2)}) async-start(bf16[16,64,1024]{2,1,0:T(8,128)(2,1)} %bitcast.67), calls=%async_computation.1 | async-start | bytes 4194304 | tf_op jit(solution)/shard_map/all_to_all | solution.py:96
  141.4 3.8 %copy-start.10 = (bf16[1,704,1024]{2,1,0:T(8,128)(2,1)S(1)}, bf16[1,704,1024]{2,1,0:T(8,128)(2,1)}, u32[]{:S(2)}) copy-start(bf16[1,704,1024]{2,1,0:T(8,128)(2,1)} %param.18) | copy-start | bytes 4325380
  141.4 3.8 %copy-start.13 = (bf16[1024,704]{0,1:T(8,128)(2,1)S(1)}, bf16[1024,704]{0,1:T(8,128)(2,1)}, u32[]{:S(2)}) copy-start(bf16[1024,704]{0,1:T(8,128)(2,1)} %get-tuple-element.8) | copy-start | bytes 4325380
  182.3 52.3 %all-to-all-start.4 = ((bf16[16,64,1024]{2,1,0:T(8,128)(2,1)}), bf16[16,64,1024]{2,1,0:T(8,128)(2,1)}, u32[]{:S(2)}, u32[]{:S(2)}) async-start(bf16[16,64,1024]{2,1,0:T(8,128)(2,1)} %bitcast.66), calls=%async_computation.5 | async-start | bytes 4194304 | tf_op jit(solution)/shard_map/all_to_all | solution.py:112
  193.6 76.7 %reduce-scatter.5.cloned.1.call-start = ((), (), s32[]{:S(2)}) async-start(), calls=%async_computation.10 | async-start | bytes 393216 | tf_op jit(solution)/shard_map/reduce_scatter | solution.py:123
  197.6 4.9 %copy-start.8 = (bf16[16,64,1024]{2,1,0:T(8,128)(2,1)S(1)}, bf16[16,64,1024]{2,1,0:T(8,128)(2,1)}, u32[]{:S(2)}) copy-start(bf16[16,64,1024]{2,1,0:T(8,128)(2,1)} %all-gather.3.cloned.1.call-done) | copy-start | bytes 6291460
  197.6 4.9 %copy-start.12 = (bf16[1024,704]{0,1:T(8,128)(2,1)S(1)}, bf16[1024,704]{0,1:T(8,128)(2,1)}, u32[]{:S(2)}) copy-start(bf16[1024,704]{0,1:T(8,128)(2,1)} %get-tuple-element.9) | copy-start | bytes 4325380
  234.6 6.6 %copy-start.1 = (bf16[768,1024]{1,0:T(8,128)(2,1)S(1)}, bf16[768,1024]{1,0:T(8,128)(2,1)}, u32[]{:S(2)}) copy-start(bf16[768,1024]{1,0:T(8,128)(2,1)} %gather_fusion.1) | copy-start | bytes 4718596
  234.6 6.6 %copy-start.6 = (pred[768]{0:T(1024)(128)(4,1)S(1)}, pred[768]{0:T(1024)(128)(4,1)}, u32[]{:S(2)}) copy-start(pred[768]{0:T(1024)(128)(4,1)} %compare_and_fusion) | copy-start | bytes 2308
  248.7 32.0 %reduce-scatter.3.cloned.1.call-start = ((), (), s32[]{:S(2)}) async-start(), calls=%async_computation.8 | async-start | bytes 393216 | tf_op jit(solution)/shard_map/reduce_scatter | solution.py:106
  256.9 4.8 %copy-start.4 = (bf16[128,1024]{1,0:T(8,128)(2,1)S(1)}, bf16[128,1024]{1,0:T(8,128)(2,1)}, u32[]{:S(2)}) copy-start(bf16[128,1024]{1,0:T(8,128)(2,1)} %param.13) | copy-start | bytes 786436
Sparse Core Ops, SparseCore 0:
  56.5 33.4 all-gather.2
  91.6 33.0 all-gather.4
  248.8 17.3 reduce-scatter.4
  268.9 11.7 reduce-scatter.2
where the time goes:
time: 288 us; the launch traced here: 287 us
  waiting for transfers between devices  79.6 us (28%)
  blocking collectives  78.5 us (27%)
  local copies, waits for them, and re-layouts  43.1 us (15%)
  matrix products  41.2 us (14%)
  starting transfers between devices  17.3 us (6%)
  between operations  14 us (5%)
  other arithmetic  13.5 us (5%)
    all_to_all x1, waiting for transfers between devices, body(): lax.all_to_all(partial_out.reshape(sources, capacity, width), 'expert', s...  33.8 us
    all_to_all x1, blocking collectives, body(): lax.all_to_all(fill_rows(x_share), 'expert', split_axis=0, concat_axis=0,...  32.1 us
    all_to_all x1, blocking collectives, body(): lax.all_to_all(fill_rows(dy_share), 'expert', split_axis=0, concat_axis=0...  29.6 us
    all_to_all x1, waiting for transfers between devices, body(): lax.all_to_all(partial_back.reshape(sources, capacity, width), 'expert',...  25.7 us
    all_to_all x1, starting transfers between devices, body(): lax.all_to_all(partial_back.reshape(sources, capacity, width), 'expert',...  11.3 us
    all_to_all x1, blocking collectives, body(): lax.all_to_all(gate_slot, 'expert', split_axis=0, concat_axis=0, tiled=True)  11.2 us
    reduce_scatter x1, waiting for transfers between devices, body(): lax.psum_scatter(mixed_part.astype(jnp.bfloat16), 'pipe', scatter_dimensi...  10.4 us
    gather x2, local copies, waits for them, and re-layouts, pick_rows(): jnp.take(flat_back, flat_slot, axis=0)  10.1 us
  transfers between devices with their start and end apart: 6, of which 4 were waited for; matrix products, arithmetic and copies ran while one was open for 19% of the time, Pallas kernels for 0%

commit v1 on v0

--- a/solution.py
+++ b/solution.py
@@ -2,6 +2,28 @@
 import jax.numpy as jnp
 from jax import lax
 from jax.sharding import PartitionSpec as P
+
+
+def in_blocks(shard, dim, count):
+    before, after = (shard.shape[:dim], shard.shape[dim + 1 :])
+    return jnp.moveaxis(shard.reshape(*before, count, -1, *after), dim, 0)
+
+
+def joined_along(pieces, dim):
+    dims = list(pieces.shape[1:])
+    dims[dim] *= pieces.shape[0]
+    return jnp.moveaxis(pieces, 0, dim).reshape(dims)
+
+
+def rotated_exchange(x, axis, split_dim, concat_dim):
+    count, index = (lax.axis_size(axis), lax.axis_index(axis))
+    tiles = in_blocks(x, split_dim, count)
+    done = [tiles[index]]
+    for step in range(1, count):
+        sent = tiles[(index + step) % count]
+        done.append(lax.ppermute(sent, axis, [(i, (i + step) % count) for i in range(count)]))
+    tiles = jnp.stack(done)[(index - jnp.arange(count)) % count]
+    return joined_along(tiles, concat_dim)
 
 
 def expert_forward(arrived_x, gate_w, up_w, down_w):
@@ -73,7 +95,7 @@
     x_share = lax.dynamic_slice_in_dim(tokens, begin, share, 1)
     dy_share = lax.dynamic_slice_in_dim(out_grad, begin, share, 1)
     part_x, part_dy, arrived_g = (
-        lax.all_to_all(fill_rows(x_share), "expert", split_axis=0, concat_axis=0, tiled=True),
+        rotated_exchange(fill_rows(x_share), "expert", 0, 0),
         lax.all_to_all(fill_rows(dy_share), "expert", split_axis=0, concat_axis=0, tiled=True),
         lax.all_to_all(gate_slot, "expert", split_axis=0, concat_axis=0, tiled=True),
     )

time: 288 us -> 327 us (1.14)
  waiting for transfers between devices: 79.6 us -> 136 us
  blocking collectives: 78.5 us -> 49.5 us
  starting transfers between devices: 17.3 us -> 27.7 us
    ppermute x0 -> x15, waiting for transfers between devices: none -> 55.9 us  [rotated_exchange(): lax.ppermute(sent, axis, [(i, (i + step) % count) for i in range(count)])]
    all_to_all x1 -> x0, blocking collectives: 32.1 us -> none  [body(): lax.all_to_all(fill_rows(x_share), 'expert', split_axis=0, concat_axis=0,...]
    ppermute x0 -> x15, starting transfers between devices: none -> 10.4 us  [rotated_exchange(): lax.ppermute(sent, axis, [(i, (i + step) % count) for i in range(count)])]
  transfers between devices with their start and end apart: 6 -> 21, of which waited for: 4 -> 15; matrix products, arithmetic and copies ran while one was open for 19% -> 17% of each run, Pallas kernels for 0% -> 0%
where the time goes in v1:
time: 327 us
  waiting for transfers between devices  136 us (42%)
  blocking collectives  49.5 us (15%)
  local copies, waits for them, and re-layouts  44.8 us (14%)
  matrix products  41.2 us (13%)
  starting transfers between devices  27.7 us (8%)
  between operations  14.3 us (4%)
  other arithmetic  13.5 us (4%)
    ppermute x15, waiting for transfers between devices, rotated_exchange(): lax.ppermute(sent, axis, [(i, (i + step) % count) for i in range(count)])  55.9 us
    all_to_all x1, waiting for transfers between devices, body(): lax.all_to_all(partial_out.reshape(sources, capacity, width), 'expert', s...  33.8 us
    all_to_all x1, blocking collectives, body(): lax.all_to_all(fill_rows(dy_share), 'expert', split_axis=0, concat_axis=0...  32.7 us
    all_to_all x1, waiting for transfers between devices, body(): lax.all_to_all(partial_back.reshape(sources, capacity, width), 'expert',...  25.8 us
    all_to_all x1, starting transfers between devices, body(): lax.all_to_all(partial_back.reshape(sources, capacity, width), 'expert',...  11.3 us
    all_to_all x1, blocking collectives, body(): lax.all_to_all(gate_slot, 'expert', split_axis=0, concat_axis=0, tiled=True)  11.2 us
    ppermute x15, starting transfers between devices, rotated_exchange(): lax.ppermute(sent, axis, [(i, (i + step) % count) for i in range(count)])  10.4 us
    reduce_scatter x1, waiting for transfers between devices, body(): lax.psum_scatter(mixed_part.astype(jnp.bfloat16), 'pipe', scatter_dimensi...  10.4 us
  transfers between devices with their start and end apart: 21, of which 15 were waited for; matrix products, arithmetic and copies ran while one was open for 17% of the time, Pallas kernels for 0%

profile of v1, /device:TPU:0, one launch (start us, length us, event | category | flops | bytes accessed | tf_op | source)
XLA Modules:
  0.0 326.7 jit_solution(11520756220992197344)
XLA Ops:
  8.6 3.4 %scatter_custom_fusion = s32[1024]{0:T(1024)S(1)} fusion(s32[768]{0:T(1024)S(1)} %fusion.23, s32[768]{0:T(1024)S(1)} %add_select_fusion, s32[]{:T(128)} %constant.138.clone.1), kind=kCustom, calls=%fused_computation.96 | custom fusion | bytes 4100 | tf_op jit(solution)/shard_map/scatter | solution.py:81
  12.0 1.0 constant_dynamic-slice_fusion
  13.0 4.0 %gather_fusion.3 = bf16[1024,512]{1,0:T(8,128)(2,1)S(1)} fusion(bf16[128,512]{1,0:T(8,128)(2,1)S(1)} %get-tuple-element.31, s32[1024]{0:T(1024)S(1)} %fusion.22), kind=kCustom, calls=%fused_computation.2.clone | custom fusion | bytes 2101248 | tf_op jit(solution)/shard_map/jit(_take)/gather | solution.py:92
  17.0 5.1 %gather_fusion.1 = bf16[1024,512]{1,0:T(8,128)(2,1)} fusion(bf16[128,512]{1,0:T(8,128)(2,1)S(1)} %get-tuple-element.32, s32[1024]{0:T(1024)S(1)} %fusion.22), kind=kCustom, calls=%fused_computation.clone | custom fusion | bytes 2101248 | tf_op jit(solution)/shard_map/jit(_take)/gather | solution.py:92
  22.1 2.4 broadcast_select_fusion.2
  24.6 5.5 %collective-permute-start.14 = (bf16[1,64,512]{2,1,0:T(8,128)(2,1)S(1)}, bf16[1,64,512]{2,1,0:T(8,128)(2,1)S(1)}, u32[]{:S(2)}, u32[]{:S(2)}) collective-permute-start(bf16[1,64,512]{2,1,0:T(8,128)(2,1)S(1)} %get-tuple-element.11), channel_id=1, source_target_pairs={{0,15},{1,0},{2,1},{3,2},{4,3},{5,4},{6,5},{7,6},{8,7},{9,8},{10,9... | collective-permute-start | bytes 196616 | tf_op jit(solution)/shard_map/ppermute | solution.py:24
  32.3 5.5 %collective-permute-done = bf16[1,64,512]{2,1,0:T(8,128)(2,1)S(1)} collective-permute-done((bf16[1,64,512]{2,1,0:T(8,128)(2,1)S(1)}, bf16[1,64,512]{2,1,0:T(8,128)(2,1)S(1)}, u32[]{:S(2)}, u32[]{:S(2)}) %collective-permute-start) | collective-permute-done | bytes 65568 | tf_op jit(solution)/shard_map/ppermute | solution.py:24
  37.8 7.0 %collective-permute-done.1 = bf16[1,64,512]{2,1,0:T(8,128)(2,1)S(1)} collective-permute-done((bf16[1,64,512]{2,1,0:T(8,128)(2,1)S(1)}, bf16[1,64,512]{2,1,0:T(8,128)(2,1)S(1)}, u32[]{:S(2)}, u32[]{:S(2)}) %collective-permute-start.1) | collective-permute-done | bytes 65568 | tf_op jit(solution)/shard_map/ppermute | solution.py:24
  44.8 5.5 %collective-permute-done.2 = bf16[1,64,512]{2,1,0:T(8,128)(2,1)S(1)} collective-permute-done((bf16[1,64,512]{2,1,0:T(8,128)(2,1)S(1)}, bf16[1,64,512]{2,1,0:T(8,128)(2,1)S(1)}, u32[]{:S(2)}, u32[]{:S(2)}) %collective-permute-start.2) | collective-permute-done | bytes 65568 | tf_op jit(solution)/shard_map/ppermute | solution.py:24
  50.3 6.1 %collective-permute-done.3 = bf16[1,64,512]{2,1,0:T(8,128)(2,1)S(1)} collective-permute-done((bf16[1,64,512]{2,1,0:T(8,128)(2,1)S(1)}, bf16[1,64,512]{2,1,0:T(8,128)(2,1)S(1)}, u32[]{:S(2)}, u32[]{:S(2)}) %collective-permute-start.3) | collective-permute-done | bytes 65568 | tf_op jit(solution)/shard_map/ppermute | solution.py:24
  56.3 5.5 %collective-permute-done.4 = bf16[1,64,512]{2,1,0:T(8,128)(2,1)S(1)} collective-permute-done((bf16[1,64,512]{2,1,0:T(8,128)(2,1)S(1)}, bf16[1,64,512]{2,1,0:T(8,128)(2,1)S(1)}, u32[]{:S(2)}, u32[]{:S(2)}) %collective-permute-start.4) | collective-permute-done | bytes 65568 | tf_op jit(solution)/shard_map/ppermute | solution.py:24
  61.8 6.1 %collective-permute-done.5 = bf16[1,64,512]{2,1,0:T(8,128)(2,1)S(1)} collective-permute-done((bf16[1,64,512]{2,1,0:T(8,128)(2,1)S(1)}, bf16[1,64,512]{2,1,0:T(8,128)(2,1)S(1)}, u32[]{:S(2)}, u32[]{:S(2)}) %collective-permute-start.5) | collective-permute-done | bytes 65568 | tf_op jit(solution)/shard_map/ppermute | solution.py:24
  67.9 4.6 %collective-permute-done.6 = bf16[1,64,512]{2,1,0:T(8,128)(2,1)S(1)} collective-permute-done((bf16[1,64,512]{2,1,0:T(8,128)(2,1)S(1)}, bf16[1,64,512]{2,1,0:T(8,128)(2,1)S(1)}, u32[]{:S(2)}, u32[]{:S(2)}) %collective-permute-start.6) | collective-permute-done | bytes 65568 | tf_op jit(solution)/shard_map/ppermute | solution.py:24
  72.5 5.2 %collective-permute-done.7 = bf16[1,64,512]{2,1,0:T(8,128)(2,1)S(1)} collective-permute-done((bf16[1,64,512]{2,1,0:T(8,128)(2,1)S(1)}, bf16[1,64,512]{2,1,0:T(8,128)(2,1)S(1)}, u32[]{:S(2)}, u32[]{:S(2)}) %collective-permute-start.7) | collective-permute-done | bytes 65568 | tf_op jit(solution)/shard_map/ppermute | solution.py:24
  77.6 4.6 %collective-permute-done.8 = bf16[1,64,512]{2,1,0:T(8,128)(2,1)S(1)} collective-permute-done((bf16[1,64,512]{2,1,0:T(8,128)(2,1)S(1)}, bf16[1,64,512]{2,1,0:T(8,128)(2,1)S(1)}, u32[]{:S(2)}, u32[]{:S(2)}) %collective-permute-start.8) | collective-permute-done | bytes 65568 | tf_op jit(solution)/shard_map/ppermute | solution.py:24
  82.2 1.8 collective-permute-start.9
  84.0 3.3 %collective-permute-done.9 = bf16[1,64,512]{2,1,0:T(8,128)(2,1)S(1)} collective-permute-done((bf16[1,64,512]{2,1,0:T(8,128)(2,1)S(1)}, bf16[1,64,512]{2,1,0:T(8,128)(2,1)S(1)}, u32[]{:S(2)}, u32[]{:S(2)}) %collective-permute-start.9) | collective-permute-done | bytes 65568 | tf_op jit(solution)/shard_map/ppermute | solution.py:24
  88.3 2.8 collective-permute-done.10
  91.2 1.6 gather_fusion
  92.8 32.7 %all_to_all.25 = bf16[16,64,512]{2,1,0:T(8,128)(2,1)} all-to-all(bf16[16,64,512]{2,1,0:T(8,128)(2,1)S(1)} %bitcast.127), channel_id=1, replica_groups=mesh['pipe'=2,'expert'=16] {'expert'}, dimensions={0} | all-to-all | bytes 2097152 | tf_op jit(solution)/shard_map/all_to_all | solution.py:99
  125.9 8.6 %scatter_custom_fusion.1 = bf16[1024]{0:T(1024)(128)(2,1)S(1)} fusion(s32[768]{0:T(1024)S(1)} %fusion.23, bf16[768]{0:T(1024)(128)(2,1)S(1)} %reshape.228, bf16[]{:T(256)} %constant.160.clone.1), kind=kCustom, calls=%fused_computation.99 | custom fusion | bytes 2050 | tf_op jit(solution)/shard_map/scatter | solution.py:85
  134.6 11.2 %all_to_all.26 = bf16[16,1,64]{2,1,0:T(2,128)(2,1)S(1)} all-to-all(bf16[16,1,64]{2,1,0:T(2,128)(2,1)S(1)} %all_to_all.20), channel_id=1, replica_groups=mesh['pipe'=2,'expert'=16] {'expert'}, dimensions={0} | all-to-all | bytes 4096 | tf_op jit(solution)/shard_map/all_to_all | solution.py:100
  145.9 5.4 %fusion.9 = f32[1024,704]{0,1:T(8,128)} fusion(bf16[1024,1024]{1,0:T(8,128)(2,1)} %bitcast.139, bf16[1,704,1024]{2,1,0:T(8,128)(2,1)} %param.18), kind=kOutput, calls=%fused_computation.29 | convolution fusion | flops 1476395008 | bytes 6422528 | tf_op jit(solution)/shard_map/dot_general | solution.py:32
  151.4 3.3 %fusion.13 = f32[1024,704]{0,1:T(8,128)} fusion(bf16[1024,1024]{1,0:T(8,128)(2,1)S(1)} %bitcast.141, bf16[1,704,1024]{2,1,0:T(8,128)(2,1)S(1)} %copy-done.9), kind=kOutput, calls=%fused_computation.33 | convolution fusion | flops 1476395008 | bytes 6422528 | tf_op jit(solution)/shard_map/dot_general | solution.py:31
  154.6 9.5 %all-gather.4.cloned.1.call-done = bf16[16,64,1024]{2,1,0:T(8,128)(2,1)} async-done(((bf16[16,64,512]{2,1,0:T(8,128)(2,1)}), bf16[16,64,1024]{2,1,0:T(8,128)(2,1)}) %all-gather.4.cloned.1.call-update) | async-done | bytes 2097168 | tf_op jit(solution)/shard_map/all_gather | solution.py:104
  164.2 2.1 multiply_convert_fusion
  166.6 5.4 %multiply_convert_fusion.1 = (bf16[1024,704]{0,1:T(8,128)(2,1)}, bf16[1024,704]{0,1:T(8,128)(2,1)}, bf16[1024,704]{0,1:T(8,128)(2,1)S(1)}) fusion(f32[1024,704]{0,1:T(8,128)} %fusion.13, f32[1024,704]{0,1:T(8,128)S(1)} %copy-done.11, bf16[1024,1024]{1,0:T(8,128)(2,1)S(1)} %bitcast.131, bf16[1,704,1024]{2,1,0:T(8,128)(2,1)S(1)} %copy-done), kind=kOutput, calls=%fused_computation.11 | convolution fusion | flops 1487208448 | bytes 13631488 | tf_op jit(solution)/shard_map/dot_general | solution.py:47
  172.0 3.2 convolution_convert_fusion
  175.2 5.6 %all-to-all-start = ((bf16[16,64,1024]{2,1,0:T(8,128)(2,1)}), bf16[16,64,1024]{2,1,0:T(8,128)(2,1)S(1)}, u32[]{:S(2)}, u32[]{:S(2)}) async-start(bf16[16,64,1024]{2,1,0:T(8,128)(2,1)} %bitcast.130), calls=%async_computation | async-start | bytes 4194304 | tf_op jit(solution)/shard_map/all_to_all | solution.py:118
  180.9 3.8 %fusion.11 = f32[1024,1024]{1,0:T(8,128)S(1)} fusion(bf16[1024,704]{0,1:T(8,128)(2,1)} %get-tuple-element.9, bf16[1,704,1024]{2,1,0:T(8,128)(2,1)} %param.17), kind=kOutput, calls=%fused_computation.31 | convolution fusion | flops 1476395008 | bytes 7077888 | tf_op jit(solution)/shard_map/dot_general | solution.py:51
  184.7 3.3 %add_convert_fusion = bf16[1024,1024]{1,0:T(8,128)(2,1)} fusion(f32[1024,1024]{1,0:T(8,128)S(1)} %fusion.11, bf16[1024,704]{0,1:T(8,128)(2,1)S(1)} %copy-done.13, bf16[1,704,1024]{2,1,0:T(8,128)(2,1)S(1)} %copy-done.10), kind=kOutput, calls=%fused_computation.9 | convolution fusion | flops 1478492160 | bytes 9175040 | tf_op jit(solution)/shard_map/dot_general | solution.py:52
  188.0 33.8 %all-to-all-done = bf16[16,64,1024]{2,1,0:T(8,128)(2,1)S(1)} async-done(((bf16[16,64,1024]{2,1,0:T(8,128)(2,1)}), bf16[16,64,1024]{2,1,0:T(8,128)(2,1)S(1)}, u32[]{:S(2)}, u32[]{:S(2)}) %all-to-all-start) | async-done | bytes 2097184 | tf_op jit(solution)/shard_map/all_to_all | solution.py:118
  221.8 11.3 %all-to-all-start.3 = ((bf16[16,64,1024]{2,1,0:T(8,128)(2,1)}), bf16[16,64,1024]{2,1,0:T(8,128)(2,1)}, u32[]{:S(2)}, u32[]{:S(2)}) async-start(bf16[16,64,1024]{2,1,0:T(8,128)(2,1)} %bitcast.129), calls=%async_computation.4 | async-start | bytes 4194304 | tf_op jit(solution)/shard_map/all_to_all | solution.py:134
  233.4 1.0 reshape.164
  237.1 4.9 %fusion.3 = bf16[1,704,1024]{2,1,0:T(8,128)(2,1)} fusion(bf16[1024,704]{0,1:T(8,128)(2,1)} %get-tuple-element.8, bf16[1024,1024]{1,0:T(8,128)(2,1)} %bitcast.140), kind=kOutput, calls=%fused_computation.23 | convolution fusion | flops 1477115904 | bytes 4980736 | tf_op jit(solution)/shard_map/dot_general | solution.py:57
  242.0 2.8 fusion.2
  244.8 3.6 %gather_fusion.2 = bf16[768,1024]{1,0:T(8,128)(2,1)} fusion(bf16[1024,1024]{1,0:T(8,128)(2,1)S(1)} %bitcast.126, s32[1024]{0:T(1024)S(1)} %pad_clamp_fusion), kind=kCustom, calls=%fused_computation.1.clone | custom fusion | bytes 3148800 | tf_op jit(solution)/shard_map/jit(_take)/gather | solution.py:69
  248.4 25.8 %all-to-all-done.3 = bf16[16,64,1024]{2,1,0:T(8,128)(2,1)} async-done(((bf16[16,64,1024]{2,1,0:T(8,128)(2,1)}), bf16[16,64,1024]{2,1,0:T(8,128)(2,1)}, u32[]{:S(2)}, u32[]{:S(2)}) %all-to-all-start.3) | async-done | bytes 2097184 | tf_op jit(solution)/shard_map/all_to_all | solution.py:134
  274.1 6.5 %gather_fusion.4 = bf16[768,1024]{1,0:T(8,128)(2,1)} fusion(bf16[1024,1024]{1,0:T(8,128)(2,1)} %bitcast.45, s32[1024]{0:T(1024)S(1)} %pad_clamp_fusion), kind=kCustom, calls=%fused_computation.3.clone | custom fusion | bytes 3148800 | tf_op jit(solution)/shard_map/jit(_take)/gather | solution.py:69
  280.7 3.5 %broadcast_select_fusion = (bf16[768,1024]{1,0:T(8,128)(2,1)}, bf16[768,1024]{1,0:T(8,128)(2,1)}) fusion(bf16[768,1024]{1,0:T(8,128)(2,1)} %gather_fusion.4, pred[768]{0:T(1024)(128)(4,1)S(1)} %copy-done.6, bf16[768,1024]{1,0:T(8,128)(2,1)S(1)} %copy-done.1), kind=kLoop, calls=%fused_computation.20 | loop fusion | flops 1572864 | bytes 6292224 | tf_op jit(solution)/shard_map/jit(_take)/select_n | solution.py:69
  284.2 2.5 reshape.170
  288.2 3.4 %fusion = bf16[1024,1024]{1,0:T(8,128)(2,1)} fusion(f32[1024]{0:T(1024)S(1)} %reshape.172, bf16[16,64,1024]{2,1,0:T(8,128)(2,1)} %all-gather.4.cloned.1.call-done), kind=kLoop, calls=%fused_computation.8 | loop fusion | flops 3145728 | bytes 4198400 | tf_op jit(solution)/shard_map/convert_element_type | solution.py:44
  291.6 2.5 reshape.165
  294.0 1.5 fusion.31
  296.4 4.8 %fusion.4 = bf16[1,704,1024]{2,1,0:T(8,128)(2,1)} fusion(bf16[1024,704]{0,1:T(8,128)(2,1)} %copy-done.14, bf16[1024,1024]{1,0:T(8,128)(2,1)} %fusion), kind=kOutput, calls=%fused_computation.24 | convolution fusion | flops 1477115904 | bytes 4980736 | tf_op jit(solution)/shard_map/dot_general | solution.py:60
  301.2 2.1 fusion.15
  304.2 5.6 %psum.7 = f32[128,6]{0,1:T(8,128)} all-reduce(f32[128,6]{0,1:T(8,128)S(1)} %bitcast.137), channel_id=1, replica_groups=mesh['pipe'=2,'expert'=16] {'pipe'}, use_global_device_ids=true, to_apply=%region_4.7 | all-reduce | flops 768 | bytes 6144 | tf_op jit(solution)/shard_map/psum | solution.py:148
  309.7 10.4 %reduce-scatter.3.cloned.1.call-done = bf16[128,512]{1,0:T(8,128)(2,1)} async-done(((bf16[128,1024]{1,0:T(8,128)(2,1)}), bf16[128,512]{1,0:T(8,128)(2,1)}) %reduce-scatter.3.cloned.1.call-update) | async-done | bytes 131088 | tf_op jit(solution)/shard_map/reduce_scatter | solution.py:128
  (96 shorter events, 11.6 us)
Async XLA Ops:
  7.2 159.1 %copy-start = (bf16[1,704,1024]{2,1,0:T(8,128)(2,1)S(1)}, bf16[1,704,1024]{2,1,0:T(8,128)(2,1)}, u32[]{:S(2)}) copy-start(bf16[1,704,1024]{2,1,0:T(8,128)(2,1)} %param.19) | copy-start | bytes 4325380
  7.2 138.7 %all-gather.6.cloned.1.call-start = ((), (), s32[]{:S(2)}) async-start(), calls=%async_computation.9 | async-start | bytes 3145728 | tf_op jit(solution)/shard_map/all_gather | solution.py:103
  8.4 3.6 %copy-start.3 = (s32[128,6]{1,0:T(8,128)}, s32[128,6]{1,0:T(8,128)S(1)}, u32[]{:S(2)}) copy-start(s32[128,6]{1,0:T(8,128)S(1)} %copy.20) | copy-start | bytes 9220
  24.6 66.6 %collective-permute-start.14 = (bf16[1,64,512]{2,1,0:T(8,128)(2,1)S(1)}, bf16[1,64,512]{2,1,0:T(8,128)(2,1)S(1)}, u32[]{:S(2)}, u32[]{:S(2)}) collective-permute-start(bf16[1,64,512]{2,1,0:T(8,128)(2,1)S(1)} %get-tuple-element.11), channel_id=1, source_target_pairs={{0,15},{1,0},{2,1},{3,2},{4,3},{5,4},{6,5},{7,6},{8,7},{9,8},{10,9... | collective-permute-start | bytes 196616 | tf_op jit(solution)/shard_map/ppermute | solution.py:24
  30.1 61.0 %collective-permute-start.13 = (bf16[1,64,512]{2,1,0:T(8,128)(2,1)S(1)}, bf16[1,64,512]{2,1,0:T(8,128)(2,1)S(1)}, u32[]{:S(2)}, u32[]{:S(2)}) collective-permute-start(bf16[1,64,512]{2,1,0:T(8,128)(2,1)S(1)} %get-tuple-element.12), channel_id=1, source_target_pairs={{0,14},{1,15},{2,0},{3,1},{4,2},{5,3},{6,4},{7,5},{8,6},{9,7},{10,... | collective-permute-start | bytes 196616 | tf_op jit(solution)/shard_map/ppermute | solution.py:24
  30.7 60.4 %collective-permute-start.12 = (bf16[1,64,512]{2,1,0:T(8,128)(2,1)S(1)}, bf16[1,64,512]{2,1,0:T(8,128)(2,1)S(1)}, u32[]{:S(2)}, u32[]{:S(2)}) collective-permute-start(bf16[1,64,512]{2,1,0:T(8,128)(2,1)S(1)} %get-tuple-element.13), channel_id=1, source_target_pairs={{0,13},{1,14},{2,15},{3,0},{4,1},{5,2},{6,3},{7,4},{8,5},{9,6},{10... | collective-permute-start | bytes 196616 | tf_op jit(solution)/shard_map/ppermute | solution.py:24
  31.0 60.1 %collective-permute-start.11 = (bf16[1,64,512]{2,1,0:T(8,128)(2,1)S(1)}, bf16[1,64,512]{2,1,0:T(8,128)(2,1)S(1)}, u32[]{:S(2)}, u32[]{:S(2)}) collective-permute-start(bf16[1,64,512]{2,1,0:T(8,128)(2,1)S(1)} %get-tuple-element.14), channel_id=1, source_target_pairs={{0,12},{1,13},{2,14},{3,15},{4,0},{5,1},{6,2},{7,3},{8,4},{9,5},{1... | collective-permute-start | bytes 196616 | tf_op jit(solution)/shard_map/ppermute | solution.py:24
  31.4 6.4 %collective-permute-start = (bf16[1,64,512]{2,1,0:T(8,128)(2,1)S(1)}, bf16[1,64,512]{2,1,0:T(8,128)(2,1)S(1)}, u32[]{:S(2)}, u32[]{:S(2)}) collective-permute-start(bf16[1,64,512]{2,1,0:T(8,128)(2,1)S(1)} %get-tuple-element.25), channel_id=1, source_target_pairs={{0,1},{1,2},{2,3},{3,4},{4,5},{5,6},{6,7},{7,8},{8,9},{9,10},{10,1... | collective-permute-start | bytes 196616 | tf_op jit(solution)/shard_map/ppermute | solution.py:24
  37.8 7.0 %collective-permute-start.1 = (bf16[1,64,512]{2,1,0:T(8,128)(2,1)S(1)}, bf16[1,64,512]{2,1,0:T(8,128)(2,1)S(1)}, u32[]{:S(2)}, u32[]{:S(2)}) collective-permute-start(bf16[1,64,512]{2,1,0:T(8,128)(2,1)S(1)} %get-tuple-element.24), channel_id=1, source_target_pairs={{0,2},{1,3},{2,4},{3,5},{4,6},{5,7},{6,8},{7,9},{8,10},{9,11},{10,... | collective-permute-start | bytes 196616 | tf_op jit(solution)/shard_map/ppermute | solution.py:24
  44.8 5.5 %collective-permute-start.2 = (bf16[1,64,512]{2,1,0:T(8,128)(2,1)S(1)}, bf16[1,64,512]{2,1,0:T(8,128)(2,1)S(1)}, u32[]{:S(2)}, u32[]{:S(2)}) collective-permute-start(bf16[1,64,512]{2,1,0:T(8,128)(2,1)S(1)} %get-tuple-element.23), channel_id=1, source_target_pairs={{0,3},{1,4},{2,5},{3,6},{4,7},{5,8},{6,9},{7,10},{8,11},{9,12},{10... | collective-permute-start | bytes 196616 | tf_op jit(solution)/shard_map/ppermute | solution.py:24
  50.2 6.1 %collective-permute-start.3 = (bf16[1,64,512]{2,1,0:T(8,128)(2,1)S(1)}, bf16[1,64,512]{2,1,0:T(8,128)(2,1)S(1)}, u32[]{:S(2)}, u32[]{:S(2)}) collective-permute-start(bf16[1,64,512]{2,1,0:T(8,128)(2,1)S(1)} %get-tuple-element.22), channel_id=1, source_target_pairs={{0,4},{1,5},{2,6},{3,7},{4,8},{5,9},{6,10},{7,11},{8,12},{9,13},{1... | collective-permute-start | bytes 196616 | tf_op jit(solution)/shard_map/ppermute | solution.py:24
  56.3 5.5 %collective-permute-start.4 = (bf16[1,64,512]{2,1,0:T(8,128)(2,1)S(1)}, bf16[1,64,512]{2,1,0:T(8,128)(2,1)S(1)}, u32[]{:S(2)}, u32[]{:S(2)}) collective-permute-start(bf16[1,64,512]{2,1,0:T(8,128)(2,1)S(1)} %get-tuple-element.21), channel_id=1, source_target_pairs={{0,5},{1,6},{2,7},{3,8},{4,9},{5,10},{6,11},{7,12},{8,13},{9,14},{... | collective-permute-start | bytes 196616 | tf_op jit(solution)/shard_map/ppermute | solution.py:24
  61.8 6.1 %collective-permute-start.5 = (bf16[1,64,512]{2,1,0:T(8,128)(2,1)S(1)}, bf16[1,64,512]{2,1,0:T(8,128)(2,1)S(1)}, u32[]{:S(2)}, u32[]{:S(2)}) collective-permute-start(bf16[1,64,512]{2,1,0:T(8,128)(2,1)S(1)} %get-tuple-element.20), channel_id=1, source_target_pairs={{0,6},{1,7},{2,8},{3,9},{4,10},{5,11},{6,12},{7,13},{8,14},{9,15},... | collective-permute-start | bytes 196616 | tf_op jit(solution)/shard_map/ppermute | solution.py:24
  67.9 4.6 %collective-permute-start.6 = (bf16[1,64,512]{2,1,0:T(8,128)(2,1)S(1)}, bf16[1,64,512]{2,1,0:T(8,128)(2,1)S(1)}, u32[]{:S(2)}, u32[]{:S(2)}) collective-permute-start(bf16[1,64,512]{2,1,0:T(8,128)(2,1)S(1)} %get-tuple-element.19), channel_id=1, source_target_pairs={{0,7},{1,8},{2,9},{3,10},{4,11},{5,12},{6,13},{7,14},{8,15},{9,0},... | collective-permute-start | bytes 196616 | tf_op jit(solution)/shard_map/ppermute | solution.py:24
  72.5 5.2 %collective-permute-start.7 = (bf16[1,64,512]{2,1,0:T(8,128)(2,1)S(1)}, bf16[1,64,512]{2,1,0:T(8,128)(2,1)S(1)}, u32[]{:S(2)}, u32[]{:S(2)}) collective-permute-start(bf16[1,64,512]{2,1,0:T(8,128)(2,1)S(1)} %get-tuple-element.18), channel_id=1, source_target_pairs={{0,8},{1,9},{2,10},{3,11},{4,12},{5,13},{6,14},{7,15},{8,0},{9,1},... | collective-permute-start | bytes 196616 | tf_op jit(solution)/shard_map/ppermute | solution.py:24
  77.6 15.2 %copy-start.2 = (bf16[1024,512]{1,0:T(8,128)(2,1)S(1)}, bf16[1024,512]{1,0:T(8,128)(2,1)}, u32[]{:S(2)}) copy-start(bf16[1024,512]{1,0:T(8,128)(2,1)} %get-tuple-element.29) | copy-start | bytes 3145732
  77.6 4.6 %collective-permute-start.8 = (bf16[1,64,512]{2,1,0:T(8,128)(2,1)S(1)}, bf16[1,64,512]{2,1,0:T(8,128)(2,1)S(1)}, u32[]{:S(2)}, u32[]{:S(2)}) collective-permute-start(bf16[1,64,512]{2,1,0:T(8,128)(2,1)S(1)} %get-tuple-element.17), channel_id=1, source_target_pairs={{0,9},{1,10},{2,11},{3,12},{4,13},{5,14},{6,15},{7,0},{8,1},{9,2},... | collective-permute-start | bytes 196616 | tf_op jit(solution)/shard_map/ppermute | solution.py:24
  82.2 5.2 %collective-permute-start.9 = (bf16[1,64,512]{2,1,0:T(8,128)(2,1)S(1)}, bf16[1,64,512]{2,1,0:T(8,128)(2,1)S(1)}, u32[]{:S(2)}, u32[]{:S(2)}) collective-permute-start(bf16[1,64,512]{2,1,0:T(8,128)(2,1)S(1)} %get-tuple-element.16), channel_id=1, source_target_pairs={{0,10},{1,11},{2,12},{3,13},{4,14},{5,15},{6,0},{7,1},{8,2},{9,3},... | collective-permute-start | bytes 196616 | tf_op jit(solution)/shard_map/ppermute | solution.py:24
  87.4 3.7 %collective-permute-start.10 = (bf16[1,64,512]{2,1,0:T(8,128)(2,1)S(1)}, bf16[1,64,512]{2,1,0:T(8,128)(2,1)S(1)}, u32[]{:S(2)}, u32[]{:S(2)}) collective-permute-start(bf16[1,64,512]{2,1,0:T(8,128)(2,1)S(1)} %get-tuple-element.15), channel_id=1, source_target_pairs={{0,11},{1,12},{2,13},{3,14},{4,15},{5,0},{6,1},{7,2},{8,3},{9,4},{... | collective-permute-start | bytes 196616 | tf_op jit(solution)/shard_map/ppermute | solution.py:24
  92.8 32.8 %copy-start.5 = (bf16[128,6]{0,1:T(8,128)(2,1)S(1)}, bf16[128,6]{0,1:T(8,128)(2,1)}, u32[]{:S(2)}) copy-start(bf16[128,6]{0,1:T(8,128)(2,1)} %param.16) | copy-start | bytes 4612
  92.8 71.4 %all-gather.4.cloned.1.call-start = ((), (), s32[]{:S(2)}) async-start(), calls=%async_computation.7 | async-start | bytes 3145728 | tf_op jit(solution)/shard_map/all_gather | solution.py:104
  145.9 5.5 %copy-start.7 = (bf16[16,64,1024]{2,1,0:T(8,128)(2,1)S(1)}, bf16[16,64,1024]{2,1,0:T(8,128)(2,1)}, u32[]{:S(2)}) copy-start(bf16[16,64,1024]{2,1,0:T(8,128)(2,1)} %all-gather.6.cloned.1.call-done) | copy-start | bytes 6291460
  145.9 5.5 %copy-start.9 = (bf16[1,704,1024]{2,1,0:T(8,128)(2,1)S(1)}, bf16[1,704,1024]{2,1,0:T(8,128)(2,1)}, u32[]{:S(2)}) copy-start(bf16[1,704,1024]{2,1,0:T(8,128)(2,1)} %param.17) | copy-start | bytes 4325380
  164.2 2.4 copy-start.11
  172.0 3.2 copy-start.14
  175.2 46.6 %all-to-all-start = ((bf16[16,64,1024]{2,1,0:T(8,128)(2,1)}), bf16[16,64,1024]{2,1,0:T(8,128)(2,1)S(1)}, u32[]{:S(2)}, u32[]{:S(2)}) async-start(bf16[16,64,1024]{2,1,0:T(8,128)(2,1)} %bitcast.130), calls=%async_computation | async-start | bytes 4194304 | tf_op jit(solution)/shard_map/all_to_all | solution.py:118
  180.9 3.8 %copy-start.10 = (bf16[1,704,1024]{2,1,0:T(8,128)(2,1)S(1)}, bf16[1,704,1024]{2,1,0:T(8,128)(2,1)}, u32[]{:S(2)}) copy-start(bf16[1,704,1024]{2,1,0:T(8,128)(2,1)} %param.18) | copy-start | bytes 4325380
  180.9 3.8 %copy-start.13 = (bf16[1024,704]{0,1:T(8,128)(2,1)S(1)}, bf16[1024,704]{0,1:T(8,128)(2,1)}, u32[]{:S(2)}) copy-start(bf16[1024,704]{0,1:T(8,128)(2,1)} %get-tuple-element.8) | copy-start | bytes 4325380
  221.8 52.3 %all-to-all-start.3 = ((bf16[16,64,1024]{2,1,0:T(8,128)(2,1)}), bf16[16,64,1024]{2,1,0:T(8,128)(2,1)}, u32[]{:S(2)}, u32[]{:S(2)}) async-start(bf16[16,64,1024]{2,1,0:T(8,128)(2,1)} %bitcast.129), calls=%async_computation.4 | async-start | bytes 4194304 | tf_op jit(solution)/shard_map/all_to_all | solution.py:134
  233.1 76.6 %reduce-scatter.5.cloned.1.call-start = ((), (), s32[]{:S(2)}) async-start(), calls=%async_computation.8 | async-start | bytes 393216 | tf_op jit(solution)/shard_map/reduce_scatter | solution.py:145
  237.1 4.9 %copy-start.8 = (bf16[16,64,1024]{2,1,0:T(8,128)(2,1)S(1)}, bf16[16,64,1024]{2,1,0:T(8,128)(2,1)}, u32[]{:S(2)}) copy-start(bf16[16,64,1024]{2,1,0:T(8,128)(2,1)} %all-gather.6.cloned.1.call-done) | copy-start | bytes 6291460
  237.1 4.9 %copy-start.12 = (bf16[1024,704]{0,1:T(8,128)(2,1)S(1)}, bf16[1024,704]{0,1:T(8,128)(2,1)}, u32[]{:S(2)}) copy-start(bf16[1024,704]{0,1:T(8,128)(2,1)} %get-tuple-element.9) | copy-start | bytes 4325380
  274.1 6.5 %copy-start.1 = (bf16[768,1024]{1,0:T(8,128)(2,1)S(1)}, bf16[768,1024]{1,0:T(8,128)(2,1)}, u32[]{:S(2)}) copy-start(bf16[768,1024]{1,0:T(8,128)(2,1)} %gather_fusion.2) | copy-start | bytes 4718596
  274.1 6.5 %copy-start.6 = (pred[768]{0:T(1024)(128)(4,1)S(1)}, pred[768]{0:T(1024)(128)(4,1)}, u32[]{:S(2)}) copy-start(pred[768]{0:T(1024)(128)(4,1)} %compare_and_fusion) | copy-start | bytes 2308
  288.1 32.0 %reduce-scatter.3.cloned.1.call-start = ((), (), s32[]{:S(2)}) async-start(), calls=%async_computation.6 | async-start | bytes 393216 | tf_op jit(solution)/shard_map/reduce_scatter | solution.py:128
  296.4 4.8 %copy-start.4 = (bf16[128,1024]{1,0:T(8,128)(2,1)S(1)}, bf16[128,1024]{1,0:T(8,128)(2,1)}, u32[]{:S(2)}) copy-start(bf16[128,1024]{1,0:T(8,128)(2,1)} %param.13) | copy-start | bytes 786436
Sparse Core Ops, SparseCore 0:
  92.9 36.5 all-gather.5
  131.0 33.0 all-gather.3
  288.3 17.3 reduce-scatter.4
  308.4 11.7 reduce-scatter.2
